TPU v7x, 32 devices: a whole 2x2x4 slice. The times are simulated.
32 devices in a mesh: dp: 8 (over z, core), mp: 4 (over y, x).
Axes of the slice: x: 2, y: 2, z: 4, core: 2. Of those that a mesh axis runs over, the one named last changes fastest.
Arguments:
- tokens: bfloat16 [12288, 2048], P(('dp', 'mp')), may hold values from -6 to 6
- segment_ids: int32 [16, 768], P('dp'), may hold values from 0 to 5, never falling along the last dimension, each value on 1 to 256 neighbouring positions
- query_weight: bfloat16 [2048, 2048], P(None, 'mp'), may hold values from -0.125 to 0.125
- key_weight: bfloat16 [2048, 2048], P(None, 'mp'), may hold values from -0.125 to 0.125
- value_weight: bfloat16 [2048, 2048], P(None, 'mp'), may hold values from -0.125 to 0.125
- out_weight: bfloat16 [2048, 2048], P('mp'), may hold values from -0.75 to 0.75
- up_weight: bfloat16 [2048, 8192], P(None, 'mp'), may hold values from -0.125 to 0.125
- down_weight: bfloat16 [8192, 2048], P('mp'), may hold values from -0.0625 to 0.0625
- attn_gain: float32 [2048], replicated, may hold values from 0.5 to 1.5
- mlp_gain: float32 [2048], replicated, may hold values from 0.5 to 1.5
- out_cotangent: bfloat16 [12288, 2048], P(('dp', 'mp')), may hold values from -18 to 18
Outputs:
- layer_output: bfloat16 [12288, 2048], P(('dp', 'mp'))
- tokens_grad: float32 [12288, 2048], P(('dp', 'mp'))
- query_weight_grad: float32 [2048, 2048], P('dp', 'mp')
- key_weight_grad: float32 [2048, 2048], P('dp', 'mp')
- value_weight_grad: float32 [2048, 2048], P('dp', 'mp')
- out_weight_grad: float32 [2048, 2048], P('mp', 'dp')
- up_weight_grad: float32 [2048, 8192], P('dp', 'mp')
- down_weight_grad: float32 [8192, 2048], P('mp', 'dp')
- attn_gain_grad: float32 [2048], replicated
- mlp_gain_grad: float32 [2048], replicated
Inputs may be any that keep to these rules, and one draw needn't show every extreme that they name: `segment_ids`: within each packed sequence the clip numbers never fall; each clip covers 1 to 256 tokens, and some clip covers exactly 256.
All inputs are finite; a program needn't handle non-finite values.
Results may differ from a plain program's by a relative error of at most 0.02.
Values may be sent and summed in bfloat16 or wider, within the bound.
A program may use at most 192 MiB of HBM per device.

v0:
```python
import math
import jax
import jax.numpy as jnp
from jax import lax
from jax.sharding import PartitionSpec as P

HEAD_DIM = 128
epsilon = 1e-05
masked_score = -1e30


def norm_rows(values, gain):
    centre = jnp.mean(values, axis=-1, keepdims=True)
    centred = values - centre
    spread = jnp.mean(centred * centred, axis=-1, keepdims=True)
    return centred * lax.rsqrt(spread + epsilon) * gain


def gelu_tanh(values):
    return jax.nn.gelu(values, approximate=True)


def block_allowed(segment):
    position = jnp.arange(segment.shape[0])
    return (position[None, :] <= position[:, None]) & (segment[:, None] == segment[None, :])


def rows_times(left_rows, right_matrix):
    return jnp.dot(left_rows, right_matrix, preferred_element_type=jnp.float32)


def rows_times_back(left_rows, right_matrix):
    return lax.dot_general(
        left_rows, right_matrix, (((1,), (1,)), ((), ())), preferred_element_type=jnp.float32
    )


def attn_input_back(
    queries_grad, keys_grad, values_grad, query_weight, key_weight, value_weight, score_scale
):
    total_grad = rows_times_back(queries_grad, query_weight) * score_scale
    total_grad = total_grad + rows_times_back(keys_grad, key_weight)
    return total_grad + rows_times_back(values_grad, value_weight)


def attend_forward(packed):
    queries, keys_in, values_in, segment = packed
    scores = jnp.einsum("qhd,khd->hqk", queries, keys_in, preferred_element_type=jnp.float32)
    scores = jnp.where(block_allowed(segment)[None], scores, masked_score)
    row_max = jnp.max(scores, axis=-1, keepdims=True)
    expanded = jnp.exp(scores - row_max)
    row_total = jnp.sum(expanded, axis=-1, keepdims=True)
    probs_low = (expanded / row_total).astype(jnp.bfloat16)
    context = jnp.einsum("hqk,khd->qhd", probs_low, values_in, preferred_element_type=jnp.float32)
    return (context.astype(jnp.bfloat16), (row_max + jnp.log(row_total))[:, :, 0])


def attend_backward(packed):
    queries, keys_in, values_in, segment, context_grad, log_total = packed
    scores = jnp.einsum("qhd,khd->hqk", queries, keys_in, preferred_element_type=jnp.float32)
    scores = jnp.where(block_allowed(segment)[None], scores, masked_score)
    attn_probs = jnp.exp(scores - log_total[:, :, None])
    probs_grad = jnp.einsum(
        "qhd,khd->hqk", context_grad, values_in, preferred_element_type=jnp.float32
    )
    values_grad = jnp.einsum(
        "hqk,qhd->khd",
        attn_probs.astype(jnp.bfloat16),
        context_grad,
        preferred_element_type=jnp.float32,
    )
    inner_sum = jnp.sum(attn_probs * probs_grad, axis=-1, keepdims=True)
    scores_grad = (attn_probs * (probs_grad - inner_sum)).astype(jnp.bfloat16)
    queries_grad = jnp.einsum(
        "hqk,khd->qhd", scores_grad, keys_in, preferred_element_type=jnp.float32
    )
    keys_grad = jnp.einsum("hqk,qhd->khd", scores_grad, queries, preferred_element_type=jnp.float32)
    return (
        queries_grad.astype(jnp.bfloat16),
        keys_grad.astype(jnp.bfloat16),
        values_grad.astype(jnp.bfloat16),
    )


def local(
    tokens,
    segment_ids,
    query_weight,
    key_weight,
    value_weight,
    out_weight,
    up_weight,
    down_weight,
    attn_gain,
    mlp_gain,
    out_cotangent,
):
    seq_count, seq_length = segment_ids.shape
    group_rows = seq_count * seq_length
    head_count = query_weight.shape[1] // HEAD_DIM
    score_scale = 1.0 / math.sqrt(HEAD_DIM)
    shaped = (seq_count, seq_length, head_count, HEAD_DIM)
    flat_shape = (group_rows, head_count * HEAD_DIM)
    residual_in = tokens.astype(jnp.float32)
    normed_attn, attn_norm_back = jax.vjp(norm_rows, residual_in, attn_gain)
    gathered_attn = lax.all_gather(normed_attn.astype(jnp.bfloat16), "mp", axis=0, tiled=True)
    queries = (
        jnp.dot(gathered_attn, query_weight, preferred_element_type=jnp.float32) * score_scale
    ).astype(jnp.bfloat16)
    keys_all = jnp.dot(gathered_attn, key_weight, preferred_element_type=jnp.float32).astype(
        jnp.bfloat16
    )
    values_all = jnp.dot(gathered_attn, value_weight, preferred_element_type=jnp.float32).astype(
        jnp.bfloat16
    )
    queries_seq = queries.reshape(shaped)
    keys_seq = keys_all.reshape(shaped)
    values_seq = values_all.reshape(shaped)
    context, log_total = lax.map(attend_forward, (queries_seq, keys_seq, values_seq, segment_ids))
    context_flat = context.reshape(flat_shape)
    attn_rows = lax.psum_scatter(
        rows_times(context_flat, out_weight).astype(jnp.bfloat16),
        "mp",
        scatter_dimension=0,
        tiled=True,
    ).astype(jnp.float32)
    residual_mid = residual_in + attn_rows
    normed_mlp, mlp_norm_back = jax.vjp(norm_rows, residual_mid, mlp_gain)
    gathered_mlp = lax.all_gather(normed_mlp.astype(jnp.bfloat16), "mp", axis=0, tiled=True)
    pre_act = jnp.dot(gathered_mlp, up_weight, preferred_element_type=jnp.float32)
    activated, gelu_back = jax.vjp(gelu_tanh, pre_act)
    hidden = activated.astype(jnp.bfloat16)
    mlp_rows = lax.psum_scatter(
        rows_times(hidden, down_weight).astype(jnp.bfloat16), "mp", scatter_dimension=0, tiled=True
    ).astype(jnp.float32)
    layer_output = (residual_mid + mlp_rows).astype(jnp.bfloat16)
    cotangent_all = lax.all_gather(out_cotangent, "mp", axis=0, tiled=True)
    down_weight_grad = jnp.einsum(
        "rf,rd->fd", hidden, cotangent_all, preferred_element_type=jnp.float32
    )
    hidden_grad = lax.dot_general(
        cotangent_all, down_weight, (((1,), (1,)), ((), ())), preferred_element_type=jnp.float32
    )
    pre_grad = gelu_back(hidden_grad)[0].astype(jnp.bfloat16)
    up_weight_grad = jnp.einsum(
        "rd,rf->df", gathered_mlp, pre_grad, preferred_element_type=jnp.float32
    )
    normed_mlp_grad = lax.psum_scatter(
        rows_times_back(pre_grad, up_weight).astype(jnp.bfloat16),
        "mp",
        scatter_dimension=0,
        tiled=True,
    ).astype(jnp.float32)
    middle_back, mlp_gain_grad = mlp_norm_back(normed_mlp_grad)
    middle_grad = out_cotangent.astype(jnp.float32) + middle_back
    middle_all_grad = lax.all_gather(middle_grad.astype(jnp.bfloat16), "mp", axis=0, tiled=True)
    out_weight_grad = jnp.einsum(
        "rc,rd->cd", context_flat, middle_all_grad, preferred_element_type=jnp.float32
    )
    context_grad = lax.dot_general(
        middle_all_grad, out_weight, (((1,), (1,)), ((), ())), preferred_element_type=jnp.float32
    ).astype(jnp.bfloat16)
    queries_grad, keys_grad, values_grad = lax.map(
        attend_backward,
        (queries_seq, keys_seq, values_seq, segment_ids, context_grad.reshape(shaped), log_total),
    )
    queries_grad = queries_grad.reshape(flat_shape)
    keys_grad = keys_grad.reshape(flat_shape)
    values_grad = values_grad.reshape(flat_shape)
    query_weight_grad = (
        jnp.einsum("rd,rc->dc", gathered_attn, queries_grad, preferred_element_type=jnp.float32)
        * score_scale
    )
    key_weight_grad = jnp.einsum(
        "rd,rc->dc", gathered_attn, keys_grad, preferred_element_type=jnp.float32
    )
    value_weight_grad = jnp.einsum(
        "rd,rc->dc", gathered_attn, values_grad, preferred_element_type=jnp.float32
    )
    normed_attn_grad = lax.psum_scatter(
        attn_input_back(
            queries_grad,
            keys_grad,
            values_grad,
            query_weight,
            key_weight,
            value_weight,
            score_scale,
        ).astype(jnp.bfloat16),
        "mp",
        scatter_dimension=0,
        tiled=True,
    ).astype(jnp.float32)
    token_back, attn_gain_grad = attn_norm_back(normed_attn_grad)
    tokens_grad = middle_grad + token_back
    attn_gain_grad, mlp_gain_grad = lax.psum((attn_gain_grad, mlp_gain_grad), ("dp", "mp"))
    (
        query_weight_grad,
        key_weight_grad,
        value_weight_grad,
        out_weight_grad,
        up_weight_grad,
        down_weight_grad,
    ) = (
        lax.psum_scatter(
            query_weight_grad.astype(jnp.bfloat16), "dp", scatter_dimension=0, tiled=True
        ).astype(jnp.float32),
        lax.psum_scatter(
            key_weight_grad.astype(jnp.bfloat16), "dp", scatter_dimension=0, tiled=True
        ).astype(jnp.float32),
        lax.psum_scatter(
            value_weight_grad.astype(jnp.bfloat16), "dp", scatter_dimension=0, tiled=True
        ).astype(jnp.float32),
        lax.psum_scatter(
            out_weight_grad.astype(jnp.bfloat16), "dp", scatter_dimension=1, tiled=True
        ).astype(jnp.float32),
        lax.psum_scatter(
            up_weight_grad.astype(jnp.bfloat16), "dp", scatter_dimension=0, tiled=True
        ).astype(jnp.float32),
        lax.psum_scatter(
            down_weight_grad.astype(jnp.bfloat16), "dp", scatter_dimension=1, tiled=True
        ).astype(jnp.float32),
    )
    return (
        layer_output,
        tokens_grad,
        query_weight_grad,
        key_weight_grad,
        value_weight_grad,
        out_weight_grad,
        up_weight_grad,
        down_weight_grad,
        attn_gain_grad,
        mlp_gain_grad,
    )


def solution(mesh):
    return jax.shard_map(
        local,
        mesh=mesh,
        in_specs=(
            P(("dp", "mp"), None),
            P("dp", None),
            P(None, "mp"),
            P(None, "mp"),
            P(None, "mp"),
            P("mp", None),
            P(None, "mp"),
            P("mp", None),
            P(),
            P(),
            P(("dp", "mp"), None),
        ),
        out_specs=(
            P(("dp", "mp"), None),
            P(("dp", "mp"), None),
            P("dp", "mp"),
            P("dp", "mp"),
            P("dp", "mp"),
            P("mp", "dp"),
            P("dp", "mp"),
            P("mp", "dp"),
            P(),
            P(),
        ),
        check_vma=False,
    )
```

profile of v0, /device:TPU:0, one launch (start us, length us, event | category | flops | bytes accessed | tf_op | source)
XLA Modules:
  0.0 1105.6 jit_solution(7210589673843302547)
XLA Ops:
  14.0 73.0 %all-gather.5.cloned.1.call-done = bf16[1536,2048]{1,0:T(8,128)(2,1)} async-done(((bf16[384,2048]{1,0:T(8,128)(2,1)}), bf16[1536,2048]{1,0:T(8,128)(2,1)}) %all-gather.5.cloned.1.call-update) | async-done | bytes 6291472 | tf_op jit(solution)/shard_map/all_gather | solution.py:106
  87.0 8.0 convolution_convert_fusion.11
  94.9 3.7 reshape.216
  98.6 2.9 copy.44
  101.6 7.3 fusion.63
  108.9 3.5 reshape.215
  112.4 2.9 copy.43
  115.3 7.3 convolution_convert_fusion.12
  122.6 3.5 reshape.214
  127.6 28.2 %while.26 = (s32[]{:T(128)}, bf16[2,768,4,128]{3,2,1,0:T(4,128)(2,1)}, f32[2,4,768]{2,1,0:T(4,128)S(1)}, bf16[2,768,4,128]{3,2,1,0:T(4,128)(2,1)}, s32[2,768]{1,...) while((s32[]{:T(128)}, ...), condition=%wide.region_5.6_spmd, body=%wide.region_2.5_spmd.sunk | while | flops 1231352832 | bytes 43362440 | solution.py:119
  130.7 2.9 select_reduce_fusion.2
  135.4 3.6 fusion.137
  144.8 2.9 select_reduce_fusion.2
  149.5 3.6 fusion.137
  155.8 7.2 convolution_convert_fusion.6
  163.8 69.6 %reduce-scatter.11.cloned.1.call-done = bf16[384,2048]{1,0:T(8,128)(2,1)} async-done(((bf16[1536,2048]{1,0:T(8,128)(2,1)}), bf16[384,2048]{1,0:T(8,128)(2,1)}) %reduce-scatter.11.cloned.1.call-update) | async-done | bytes 1572880 | tf_op jit(solution)/shard_map/reduce_scatter | solution.py:121
  233.4 2.5 fusion.65
  238.9 66.6 %all-gather.9.cloned.1.call-done = bf16[1536,2048]{1,0:T(8,128)(2,1)} async-done(((bf16[384,2048]{1,0:T(8,128)(2,1)}), bf16[1536,2048]{1,0:T(8,128)(2,1)}) %all-gather.9.cloned.1.call-update) | async-done | bytes 6291472 | tf_op jit(solution)/shard_map/all_gather | solution.py:137
  305.5 19.1 %fusion.89 = f32[1536,2048]{1,0:T(8,128)} fusion(bf16[1536,2048]{1,0:T(8,128)(2,1)} %all-gather.9.cloned.1.call-done, bf16[2048,2048]{1,0:T(8,128)(2,1)} %param.22), kind=kOutput, calls=%fused_computation.146 | convolution fusion | flops 12884901888 | bytes 27262976 | tf_op jit(solution)/shard_map/dot_general | solution.py:141
  324.5 53.4 %all-gather.7.cloned.1.call-done = bf16[1536,2048]{1,0:T(8,128)(2,1)} async-done(((bf16[384,2048]{1,0:T(8,128)(2,1)}), bf16[1536,2048]{1,0:T(8,128)(2,1)}) %all-gather.7.cloned.1.call-update) | async-done | bytes 6291472 | tf_op jit(solution)/shard_map/all_gather | solution.py:129
  377.9 29.6 %fusion.48 = (bf16[1536,2048]{1,0:T(8,128)(2,1)}, f32[1536,2048]{1,0:T(8,128)}) fusion(f32[1536,2048]{1,0:T(8,128)} %fusion.89, bf16[1536,2048]{1,0:T(8,128)(2,1)} %all-gather.7.cloned.1.call-done, bf16[2048,2048]{1,0:T(8,128)(2,1)} %param.21), kind=kOutput, calls=%fused_computation.68 | convolution fusion | flops 12947816448 | bytes 46137344 | tf_op jit(solution)/shard_map/dot_general | solution.py:130
  407.5 19.1 %convolution_convert_fusion.4 = bf16[1536,2048]{1,0:T(8,128)(2,1)} fusion(bf16[1536,2048]{1,0:T(8,128)(2,1)} %get-tuple-element.190, bf16[2048,2048]{1,0:T(8,128)(2,1)} %param.21), kind=kOutput, calls=%fused_computation.73 | convolution fusion | flops 12888047616 | bytes 20971520 | tf_op jit(solution)/shard_map/dot_general | solution.py:33
  426.7 20.5 %convolution_convert_fusion.5 = bf16[1536,2048]{1,0:T(8,128)(2,1)} fusion(bf16[2048,2048]{1,0:T(8,128)(2,1)} %param.22, f32[1536,2048]{1,0:T(8,128)} %get-tuple-element.191), kind=kOutput, calls=%fused_computation.74 | convolution fusion | flops 12916359168 | bytes 27262976 | tf_op jit(solution)/shard_map/dot_general | solution.py:29
  447.3 49.7 %reduce-scatter.15.cloned.1.call-done = bf16[384,2048]{1,0:T(8,128)(2,1)} async-done(((bf16[1536,2048]{1,0:T(8,128)(2,1)}), bf16[384,2048]{1,0:T(8,128)(2,1)}) %reduce-scatter.15.cloned.1.call-update) | async-done | bytes 1572880 | tf_op jit(solution)/shard_map/reduce_scatter | solution.py:148
  497.0 4.4 fusion.59
  501.4 68.7 %reduce-scatter.13.cloned.1.call-done = bf16[384,2048]{1,0:T(8,128)(2,1)} async-done(((bf16[1536,2048]{1,0:T(8,128)(2,1)}), bf16[384,2048]{1,0:T(8,128)(2,1)}) %reduce-scatter.13.cloned.1.call-update) | async-done | bytes 1572880 | tf_op jit(solution)/shard_map/reduce_scatter | solution.py:133
  570.1 5.5 fusion.88
  578.9 19.6 %convolution_convert_fusion.3 = bf16[2048,2048]{1,0:T(8,128)(2,1)} fusion(bf16[1536,2048]{1,0:T(8,128)(2,1)} %all-gather.7.cloned.1.call-done, bf16[1536,2048]{1,0:T(8,128)(2,1)} %get-tuple-element.190), kind=kOutput, calls=%fused_computation.72 | convolution fusion | flops 12889096192 | bytes 20971520 | tf_op jit(solution)/shard_map/rd,rf->df/dot_general | solution.py:145
  598.5 22.5 %convolution_convert_fusion.2 = bf16[2048,2048]{1,0:T(8,128)(2,1)} fusion(bf16[1536,2048]{1,0:T(8,128)(2,1)} %all-gather.9.cloned.1.call-done, f32[1536,2048]{1,0:T(8,128)} %get-tuple-element.191), kind=kOutput, calls=%fused_computation.71 | convolution fusion | flops 12917407744 | bytes 27262976 | tf_op jit(solution)/shard_map/rf,rd->fd/dot_general | solution.py:138
  621.1 28.0 %all-gather.11.cloned.1.call-done = bf16[1536,2048]{1,0:T(8,128)(2,1)} async-done(((bf16[384,2048]{1,0:T(8,128)(2,1)}), bf16[1536,2048]{1,0:T(8,128)(2,1)}) %all-gather.11.cloned.1.call-update) | async-done | bytes 6291472 | tf_op jit(solution)/shard_map/all_gather | solution.py:156
  649.1 7.8 convolution_convert_fusion.10
  657.0 3.7 reshape.218
  660.6 8.1 convolution_convert_fusion.7
  673.6 99.9 %while.27 = (s32[]{:T(128)}, bf16[2,768,4,128]{3,2,1,0:T(4,128)(2,1)}, bf16[2,768,4,128]{3,2,1,0:T(4,128)(2,1)}, bf16[2,768,4,128]{3,2,1,0:T(4,128)(2,1)}, bf16[...) while((s32[]{:T(128)}, ...), condition=%wide.region_15.16_spmd, body=%wide.region_13.15_spmd.sunk | while | flops 3051156480 | bytes 169179440 | solution.py:163
  675.9 2.3 constant_dynamic-slice_fusion.7
  679.6 3.6 copy-done.1
  683.2 3.5 fusion.148
  689.0 8.2 multiply_reduce_fusion.3
  697.2 10.9 multiply_convert_fusion.7
  708.1 4.5 fusion.149
  720.2 3.1 constant_dynamic-update-slice_fusion.9
  725.4 2.3 constant_dynamic-slice_fusion.7
  729.1 3.6 copy-done.1
  732.8 3.5 fusion.148
  738.5 8.1 multiply_reduce_fusion.3
  746.6 11.5 %multiply_convert_fusion.7 = bf16[4,768,768]{1,2,0:T(8,128)(2,1)} fusion(f32[4,768,768]{1,2,0:T(8,128)} %get-tuple-element.304, f32[4,768,768]{1,2,0:T(8,128)} %copy-done.1, f32[4,768]{1,0:T(4,128)S(1)} %get-tuple-element.305, f32[4,768]{1,0:T(4,128)S(1)} %dynamic-slice_bitcast_fusion.2, pred[768,768]{0,1:T(8,128)(4,1)S(1)} %fusion.146), kind=kLoop, calls=%fused_computation.21.clone.1 | loop fusion | flops 11796480 | bytes 24207360 | tf_op jit(solution)/shard_map/while/body/eval_jaxpr/convert_element_type | solution.py:73
  758.1 4.4 fusion.149
  770.2 3.1 constant_dynamic-update-slice_fusion.9
  773.5 8.1 multiply_convert_fusion.2
  781.7 8.1 convolution_convert_fusion.8
  789.8 8.1 convolution_convert_fusion.9
  798.3 10.2 fusion.72
  808.5 6.5 fusion.69
  815.0 15.8 %add_convert_fusion = bf16[1536,2048]{1,0:T(8,128)(2,1)} fusion(f32[1536,2048]{1,0:T(8,128)} %fusion.69, f32[1536,2048]{1,0:T(8,128)} %fusion.72, bf16[2048,512]{1,0:T(8,128)(2,1)} %param.17, bf16[192,8,4,128]{3,2,1,0:T(4,128)(2,1)} %bitcast.147), kind=kOutput, calls=%fused_computation.69 | convolution fusion | flops 3233808384 | bytes 35127296 | tf_op jit(solution)/shard_map/dot_general | solution.py:33
  830.8 2.8 convert_element_type.158
  833.6 2.7 convert_element_type.160
  836.4 31.3 %reduce-scatter.25.cloned.1.call-done = bf16[512,256]{1,0:T(8,128)(2,1)} async-done(((bf16[512,2048]{1,0:T(8,128)(2,1)}), bf16[512,256]{1,0:T(8,128)(2,1)}) %reduce-scatter.25.cloned.1.call-update) | async-done | bytes 262160 | tf_op jit(solution)/shard_map/reduce_scatter | solution.py:214
  869.4 34.9 %reduce-scatter.19.cloned.1.call-done = bf16[256,512]{1,0:T(8,128)(2,1)} async-done(((bf16[2048,512]{1,0:T(8,128)(2,1)}), bf16[256,512]{1,0:T(8,128)(2,1)}) %reduce-scatter.19.cloned.1.call-update) | async-done | bytes 262160 | tf_op jit(solution)/shard_map/reduce_scatter | solution.py:205
  906.1 34.9 %reduce-scatter.23.cloned.1.call-done = bf16[256,512]{1,0:T(8,128)(2,1)} async-done(((bf16[2048,512]{1,0:T(8,128)(2,1)}), bf16[256,512]{1,0:T(8,128)(2,1)}) %reduce-scatter.23.cloned.1.call-update) | async-done | bytes 262160 | tf_op jit(solution)/shard_map/reduce_scatter | solution.py:211
  942.9 34.9 %reduce-scatter.21.cloned.1.call-done = bf16[256,512]{1,0:T(8,128)(2,1)} async-done(((bf16[2048,512]{1,0:T(8,128)(2,1)}), bf16[256,512]{1,0:T(8,128)(2,1)}) %reduce-scatter.21.cloned.1.call-update) | async-done | bytes 262160 | tf_op jit(solution)/shard_map/reduce_scatter | solution.py:208
  979.6 70.0 %reduce-scatter.17.cloned.1.call-done = bf16[384,2048]{1,0:T(8,128)(2,1)} async-done(((bf16[1536,2048]{1,0:T(8,128)(2,1)}), bf16[384,2048]{1,0:T(8,128)(2,1)}) %reduce-scatter.17.cloned.1.call-update) | async-done | bytes 1572880 | tf_op jit(solution)/shard_map/reduce_scatter | solution.py:180
  1049.6 2.8 fusion.62
  1054.0 39.5 %all-reduce = (f32[2048]{0:T(1024)}, f32[2048]{0:T(1024)}) all-reduce(f32[2048]{0:T(1024)S(1)} %get-tuple-element.143, f32[2048]{0:T(1024)S(1)} %copy-done.27), channel_id=1, replica_groups=mesh['dp'=8,'mp'=4] {'dp','mp'}, use_global_device_ids=true, to_apply=%region_26.27 | all-reduce | flops 4096 | bytes 32768 | tf_op jit(solution)/shard_map/psum | solution.py:196
  1093.5 5.1 add_add_fusion.2
  (168 shorter events, 71.3 us)
Async XLA Ops:
  7.2 148.6 %copy-start = (bf16[512,2048]{1,0:T(8,128)(2,1)S(1)}, bf16[512,2048]{1,0:T(8,128)(2,1)}, u32[]{:S(2)}) copy-start(bf16[512,2048]{1,0:T(8,128)(2,1)} %param.20) | copy-start | bytes 6291460
  7.2 5.0 copy-start.20
  7.2 79.8 %all-gather.5.cloned.1.call-start = ((), (), s32[]{:S(2)}) async-start(), calls=%async_computation.10 | async-start | bytes 7864320 | tf_op jit(solution)/shard_map/all_gather | solution.py:106
  7.2 5.0 copy-start.3
  9.1 2.5 copy-start.22
  11.1 0.6 copy-start.30
  11.7 0.6 copy-start.25
  13.9 219.5 %reduce-scatter.11.cloned.1.call-start = ((), (), s32[]{:S(2)}) async-start(), calls=%async_computation.11 | async-start | bytes 7864320 | tf_op jit(solution)/shard_map/reduce_scatter | solution.py:121
  98.6 2.9 copy-start.14
  112.4 2.9 copy-start.32
  122.6 5.1 copy-start.18
  133.6 1.8 copy-start.11
  147.7 1.8 copy-start.11
  155.8 7.2 copy-start.16
  163.1 142.4 %all-gather.9.cloned.1.call-start = ((), (), s32[]{:S(2)}) async-start(), calls=%async_computation.14 | async-start | bytes 7864320 | tf_op jit(solution)/shard_map/all_gather | solution.py:137
  163.1 73.9 %copy-start.24 = (f32[2048]{0:T(1024)S(1)}, f32[2048]{0:T(1024)}, u32[]{:S(2)}) copy-start(f32[2048]{0:T(1024)} %param.24) | copy-start | bytes 24580
  163.8 214.1 %all-gather.7.cloned.1.call-start = ((), (), s32[]{:S(2)}) async-start(), calls=%async_computation.12 | async-start | bytes 7864320 | tf_op jit(solution)/shard_map/all_gather | solution.py:129
  233.4 2.5 copy-start.4
  233.4 2.8 copy-start.9
  238.8 258.2 %reduce-scatter.15.cloned.1.call-start = ((), (), s32[]{:S(2)}) async-start(), calls=%async_computation.15 | async-start | bytes 7864320 | tf_op jit(solution)/shard_map/reduce_scatter | solution.py:148
  426.7 143.4 %reduce-scatter.13.cloned.1.call-start = ((), (), s32[]{:S(2)}) async-start(), calls=%async_computation.13 | async-start | bytes 7864320 | tf_op jit(solution)/shard_map/reduce_scatter | solution.py:133
  447.2 201.9 %all-gather.11.cloned.1.call-start = ((), (), s32[]{:S(2)}) async-start(), calls=%async_computation.16 | async-start | bytes 7864320 | tf_op jit(solution)/shard_map/all_gather | solution.py:156
  570.1 7.2 copy-start.13
  575.6 1.7 copy-start.10
  575.6 1.7 copy-start.28
  578.8 252.0 %reduce-scatter.27.cloned.1.call-start = ((), (), s32[]{:S(2)}) async-start(), calls=%async_computation.22 | async-start | bytes 9437184 | tf_op jit(solution)/shard_map/reduce_scatter | solution.py:217
  598.5 235.2 %reduce-scatter.29.cloned.1.call-start = ((), (), s32[]{:S(2)}) async-start(), calls=%async_computation.23 | async-start | bytes 9437184 | tf_op jit(solution)/shard_map/reduce_scatter | solution.py:220
  621.0 246.6 %reduce-scatter.25.cloned.1.call-start = ((), (), s32[]{:S(2)}) async-start(), calls=%async_computation.21 | async-start | bytes 2359296 | tf_op jit(solution)/shard_map/reduce_scatter | solution.py:214
  668.8 4.8 copy-start.17
  668.8 4.8 copy-start.19
  668.8 235.5 %reduce-scatter.19.cloned.1.call-start = ((), (), s32[]{:S(2)}) async-start(), calls=%async_computation.18 | async-start | bytes 2359296 | tf_op jit(solution)/shard_map/reduce_scatter | solution.py:205
  673.8 4.4 copy-start.6
  673.8 4.4 copy-start.8
  679.6 3.6 copy-start.1
  708.1 4.5 copy-start.2
  708.1 4.6 copy-start.7
  723.3 4.5 copy-start.6
  723.3 4.5 copy-start.8
  729.1 3.6 copy-start.1
  758.1 4.4 copy-start.2
  758.1 4.6 copy-start.7
  781.6 159.5 %reduce-scatter.23.cloned.1.call-start = ((), (), s32[]{:S(2)}) async-start(), calls=%async_computation.20 | async-start | bytes 2359296 | tf_op jit(solution)/shard_map/reduce_scatter | solution.py:211
  789.8 188.0 %reduce-scatter.21.cloned.1.call-start = ((), (), s32[]{:S(2)}) async-start(), calls=%async_computation.19 | async-start | bytes 2359296 | tf_op jit(solution)/shard_map/reduce_scatter | solution.py:208
  798.0 251.6 %reduce-scatter.17.cloned.1.call-start = ((), (), s32[]{:S(2)}) async-start(), calls=%async_computation.17 | async-start | bytes 7864320 | tf_op jit(solution)/shard_map/reduce_scatter | solution.py:180
  798.3 10.2 copy-start.15
  798.3 10.2 copy-start.33
  833.6 215.9 %copy-start.21 = (f32[2048]{0:T(1024)S(1)}, f32[2048]{0:T(1024)}, u32[]{:S(2)}) copy-start(f32[2048]{0:T(1024)} %param.23) | copy-start | bytes 24580
  833.6 215.9 %copy-start.23 = (f32[384]{0:T(512)S(1)}, f32[384]{0:T(512)}, u32[]{:S(2)}) copy-start(f32[384]{0:T(512)} %copy-done.22) | copy-start | bytes 4612
  836.4 216.0 %copy-start.31 = (f32[384]{0:T(512)S(1)}, f32[384]{0:T(512)}, u32[]{:S(2)}) copy-start(f32[384]{0:T(512)} %copy-done.30) | copy-start | bytes 4612
  836.4 216.0 %copy-start.26 = (f32[384]{0:T(512)S(1)}, f32[384]{0:T(512)}, u32[]{:S(2)}) copy-start(f32[384]{0:T(512)} %copy-done.25) | copy-start | bytes 4612
  979.6 74.4 %copy-start.27 = (f32[2048]{0:T(1024)S(1)}, f32[2048]{0:T(1024)}, u32[]{:S(2)}) copy-start(f32[2048]{0:T(1024)} %get-tuple-element.141) | copy-start | bytes 24580
  979.6 113.9 %copy-start.29 = (f32[384]{0:T(512)S(1)}, f32[384]{0:T(512)}, u32[]{:S(2)}) copy-start(f32[384]{0:T(512)} %copy-done.28) | copy-start | bytes 4612
  1049.6 2.8 copy-start.5
  1049.6 2.8 copy-start.12
Sparse Core Ops, SparseCore 0:
  14.1 72.8 all-gather.4
  163.2 70.2 reduce-scatter.10
  235.3 70.1 all-gather.8
  307.7 70.1 all-gather.6
  426.8 70.1 reduce-scatter.14
  499.8 70.1 reduce-scatter.12
  579.0 70.1 all-gather.10
  651.4 89.5 reduce-scatter.26
  743.4 87.9 reduce-scatter.28
  833.5 34.0 reduce-scatter.24
  870.0 34.3 reduce-scatter.18
  906.5 34.5 reduce-scatter.22
  943.4 34.3 reduce-scatter.20
  980.6 68.8 reduce-scatter.16
where the time goes:
time: 1110 us
  waiting for transfers between devices  616 us (55%)
  matrix products  285 us (26%)
  local copies, waits for them, and re-layouts  78.1 us (7%)
  other arithmetic  71.6 us (6%)
  blocking collectives  39.5 us (4%)
  between operations  14.6 us (1%)
    all_gather x1, waiting for transfers between devices, local(): lax.all_gather(normed_attn.astype(jnp.bfloat16), 'mp', axis=0, tiled=True)  73 us
    reduce_scatter x1, waiting for transfers between devices, local(): lax.psum_scatter(attn_input_back(queries_grad, keys_grad, values_grad, qu...  70 us
    reduce_scatter x1, waiting for transfers between devices, local(): lax.psum_scatter(rows_times(context_flat, out_weight).astype(jnp.bfloat16...  69.6 us
    reduce_scatter x1, waiting for transfers between devices, local(): lax.psum_scatter(rows_times(hidden, down_weight).astype(jnp.bfloat16), 'm...  68.7 us
    all_gather x1, waiting for transfers between devices, local(): cotangent_all = lax.all_gather(out_cotangent, 'mp', axis=0, tiled=True)  66.6 us
    all_gather x1, waiting for transfers between devices, local(): lax.all_gather(normed_mlp.astype(jnp.bfloat16), 'mp', axis=0, tiled=True)  53.4 us
    dot_general x4, matrix products, rows_times_back(): lax.dot_general(left_rows, right_matrix, (((1,), (1,)), ((), ())), prefer...  51.6 us
    reduce_scatter x1, waiting for transfers between devices, local(): lax.psum_scatter(rows_times_back(pre_grad, up_weight).astype(jnp.bfloat16...  49.7 us
  transfers between devices with their start and end apart: 14, of which 12 were waited for; matrix products, arithmetic and copies ran while one was open for 25% of the time, Pallas kernels for 0%

commit v1 on v0

--- a/solution.py
+++ b/solution.py
@@ -7,6 +7,24 @@
 HEAD_DIM = 128
 epsilon = 1e-05
 masked_score = -1e30
+
+
+def laid_out(blocks, dim):
+    blocks = jnp.moveaxis(blocks, 0, dim)
+    dims = blocks.shape
+    return blocks.reshape(*dims[:dim], dims[dim] * dims[dim + 1], *dims[dim + 2 :])
+
+
+def collected_by_bits(x, axis):
+    size = lax.axis_size(axis)
+    tiles = x[None]
+    for level in range(size.bit_length() - 1):
+        distance = 1 << level
+        theirs = lax.ppermute(tiles, axis, [(i, i ^ distance) for i in range(size)])
+        both = jnp.stack([tiles, theirs])
+        upper = lax.axis_index(axis) >> level & 1
+        tiles = jnp.where(upper == 0, both, both[::-1]).reshape(-1, *x.shape)
+    return tiles
 
 
 def norm_rows(values, gain):
@@ -153,7 +171,8 @@
     ).astype(jnp.float32)
     middle_back, mlp_gain_grad = mlp_norm_back(normed_mlp_grad)
     middle_grad = out_cotangent.astype(jnp.float32) + middle_back
-    middle_all_grad = lax.all_gather(middle_grad.astype(jnp.bfloat16), "mp", axis=0, tiled=True)
+    x = middle_grad.astype(jnp.bfloat16)
+    middle_all_grad = laid_out(collected_by_bits(x, "mp"), 0)
     out_weight_grad = jnp.einsum(
         "rc,rd->cd", context_flat, middle_all_grad, preferred_element_type=jnp.float32
     )

time: 1110 us -> 1070 us (0.964)
  waiting for transfers between devices: 616 us -> 558 us
  other arithmetic: 71.6 us -> 85.1 us
    ppermute x0 -> x2, waiting for transfers between devices: none -> 100 us  [collected_by_bits(): theirs = lax.ppermute(tiles, axis, [(i, i ^ distance) for i in range(size)])]
    reduce_scatter x1, waiting for transfers between devices: 49.7 us -> 6.65 us  [local(): lax.psum_scatter(rows_times_back(pre_grad, up_weight).astype(jnp.bfloat16...]
    reduce_scatter x1, waiting for transfers between devices: 34.9 us -> 0.01 us  [local(): lax.psum_scatter(query_weight_grad.astype(jnp.bfloat16), 'dp', scatter_di...]
    reduce_scatter x1, waiting for transfers between devices: 31.3 us -> 0.01 us  [local(): lax.psum_scatter(out_weight_grad.astype(jnp.bfloat16), 'dp', scatter_dime...]
    all_gather x1 -> x0, waiting for transfers between devices: 28 us -> none  [local(): lax.all_gather(middle_grad.astype(jnp.bfloat16), 'mp', axis=0, tiled=True)]
    reduce_scatter x1, waiting for transfers between devices: 34.9 us -> 14.8 us  [local(): lax.psum_scatter(value_weight_grad.astype(jnp.bfloat16), 'dp', scatter_di...]
    another operation x0 -> x4, other arithmetic: none -> 11.8 us  [collected_by_bits(): both = jnp.stack([tiles, theirs])]
  transfers between devices with their start and end apart: 14 -> 15, of which waited for: 12 -> 11; matrix products, arithmetic and copies ran while one was open for 25% -> 28% of each run, Pallas kernels for 0% -> 0%
where the time goes in v1:
time: 1070 us; the launch traced here: 1060 us
  waiting for transfers between devices  558 us (52%)
  matrix products  282 us (26%)
  other arithmetic  85.1 us (8%)
  local copies, waits for them, and re-layouts  80.1 us (7%)
  blocking collectives  39.5 us (4%)
  between operations  14.6 us (1%)
    ppermute x2, waiting for transfers between devices, collected_by_bits(): theirs = lax.ppermute(tiles, axis, [(i, i ^ distance) for i in range(size)])  100 us
    all_gather x1, waiting for transfers between devices, local(): lax.all_gather(normed_attn.astype(jnp.bfloat16), 'mp', axis=0, tiled=True)  73 us
    reduce_scatter x1, waiting for transfers between devices, local(): lax.psum_scatter(attn_input_back(queries_grad, keys_grad, values_grad, qu...  70 us
    reduce_scatter x1, waiting for transfers between devices, local(): lax.psum_scatter(rows_times(context_flat, out_weight).astype(jnp.bfloat16...  69.6 us
    reduce_scatter x1, waiting for transfers between devices, local(): lax.psum_scatter(rows_times(hidden, down_weight).astype(jnp.bfloat16), 'm...  68.7 us
    all_gather x1, waiting for transfers between devices, local(): cotangent_all = lax.all_gather(out_cotangent, 'mp', axis=0, tiled=True)  65.4 us
    all_gather x1, waiting for transfers between devices, local(): lax.all_gather(normed_mlp.astype(jnp.bfloat16), 'mp', axis=0, tiled=True)  53.4 us
    dot_general x4, matrix products, rows_times_back(): lax.dot_general(left_rows, right_matrix, (((1,), (1,)), ((), ())), prefer...  51.5 us
  transfers between devices with their start and end apart: 15, of which 11 were waited for; matrix products, arithmetic and copies ran while one was open for 28% of the time, Pallas kernels for 0%

profile of v1, /device:TPU:0, one launch (start us, length us, event | category | flops | bytes accessed | tf_op | source)
XLA Modules:
  0.0 1063.2 jit_solution(14198173460387415344)
XLA Ops:
  14.0 73.0 %all-gather.4.cloned.1.call-done = bf16[1536,2048]{1,0:T(8,128)(2,1)} async-done(((bf16[384,2048]{1,0:T(8,128)(2,1)}), bf16[1536,2048]{1,0:T(8,128)(2,1)}) %all-gather.4.cloned.1.call-update) | async-done | bytes 6291472 | tf_op jit(solution)/shard_map/all_gather | solution.py:124
  87.0 8.0 convolution_convert_fusion.11
  95.0 3.7 reshape.219
  98.7 2.9 copy.44
  101.6 7.3 fusion.63
  108.9 3.5 reshape.218
  112.4 2.9 copy.43
  115.3 7.3 convolution_convert_fusion.12
  122.6 3.5 reshape.217
  127.7 28.2 %while.26 = (s32[]{:T(128)}, bf16[2,768,4,128]{3,2,1,0:T(4,128)(2,1)}, f32[2,4,768]{2,1,0:T(4,128)S(1)}, bf16[2,768,4,128]{3,2,1,0:T(4,128)(2,1)}, s32[2,768]{1,...) while((s32[]{:T(128)}, ...), condition=%wide.region_5.6_spmd, body=%wide.region_2.5_spmd.sunk | while | flops 1231352832 | bytes 43362440 | solution.py:137
  130.7 2.9 select_reduce_fusion.2
  135.4 3.6 fusion.141
  144.8 2.9 select_reduce_fusion.2
  149.5 3.6 fusion.141
  155.8 7.2 convolution_convert_fusion.6
  163.8 69.6 %reduce-scatter.11.cloned.1.call-done = bf16[384,2048]{1,0:T(8,128)(2,1)} async-done(((bf16[1536,2048]{1,0:T(8,128)(2,1)}), bf16[384,2048]{1,0:T(8,128)(2,1)}) %reduce-scatter.11.cloned.1.call-update) | async-done | bytes 1572880 | tf_op jit(solution)/shard_map/reduce_scatter | solution.py:139
  240.0 65.4 %all-gather.8.cloned.1.call-done = bf16[1536,2048]{1,0:T(8,128)(2,1)} async-done(((bf16[384,2048]{1,0:T(8,128)(2,1)}), bf16[1536,2048]{1,0:T(8,128)(2,1)}) %all-gather.8.cloned.1.call-update) | async-done | bytes 6291472 | tf_op jit(solution)/shard_map/all_gather | solution.py:155
  305.4 19.1 %fusion.91 = f32[1536,2048]{1,0:T(8,128)} fusion(bf16[1536,2048]{1,0:T(8,128)(2,1)} %all-gather.8.cloned.1.call-done, bf16[2048,2048]{1,0:T(8,128)(2,1)} %param.22), kind=kOutput, calls=%fused_computation.152 | convolution fusion | flops 12884901888 | bytes 27262976 | tf_op jit(solution)/shard_map/dot_general | solution.py:159
  324.5 53.4 %all-gather.6.cloned.1.call-done = bf16[1536,2048]{1,0:T(8,128)(2,1)} async-done(((bf16[384,2048]{1,0:T(8,128)(2,1)}), bf16[1536,2048]{1,0:T(8,128)(2,1)}) %all-gather.6.cloned.1.call-update) | async-done | bytes 6291472 | tf_op jit(solution)/shard_map/all_gather | solution.py:147
  377.9 29.6 %fusion.48 = (bf16[1536,2048]{1,0:T(8,128)(2,1)}, f32[1536,2048]{1,0:T(8,128)}) fusion(f32[1536,2048]{1,0:T(8,128)} %fusion.91, bf16[1536,2048]{1,0:T(8,128)(2,1)} %all-gather.6.cloned.1.call-done, bf16[2048,2048]{1,0:T(8,128)(2,1)} %param.21), kind=kOutput, calls=%fused_computation.68 | convolution fusion | flops 12947816448 | bytes 46137344 | tf_op jit(solution)/shard_map/dot_general | solution.py:148
  407.6 19.1 %convolution_convert_fusion.4 = bf16[1536,2048]{1,0:T(8,128)(2,1)} fusion(bf16[1536,2048]{1,0:T(8,128)(2,1)} %get-tuple-element.192, bf16[2048,2048]{1,0:T(8,128)(2,1)} %param.21), kind=kOutput, calls=%fused_computation.74 | convolution fusion | flops 12888047616 | bytes 20971520 | tf_op jit(solution)/shard_map/dot_general | solution.py:51
  426.8 20.5 %convolution_convert_fusion.5 = bf16[1536,2048]{1,0:T(8,128)(2,1)} fusion(bf16[2048,2048]{1,0:T(8,128)(2,1)} %param.22, f32[1536,2048]{1,0:T(8,128)} %get-tuple-element.193), kind=kOutput, calls=%fused_computation.75 | convolution fusion | flops 12916359168 | bytes 27262976 | tf_op jit(solution)/shard_map/dot_general | solution.py:47
  447.4 20.0 %convolution_convert_fusion.3 = bf16[2048,2048]{1,0:T(8,128)(2,1)} fusion(bf16[1536,2048]{1,0:T(8,128)(2,1)} %all-gather.6.cloned.1.call-done, bf16[1536,2048]{1,0:T(8,128)(2,1)} %get-tuple-element.192), kind=kOutput, calls=%fused_computation.73 | convolution fusion | flops 12889096192 | bytes 20971520 | tf_op jit(solution)/shard_map/rd,rf->df/dot_general | solution.py:163
  467.4 22.6 %convolution_convert_fusion.2 = bf16[2048,2048]{1,0:T(8,128)(2,1)} fusion(bf16[1536,2048]{1,0:T(8,128)(2,1)} %all-gather.8.cloned.1.call-done, f32[1536,2048]{1,0:T(8,128)} %get-tuple-element.193), kind=kOutput, calls=%fused_computation.72 | convolution fusion | flops 12917407744 | bytes 27262976 | tf_op jit(solution)/shard_map/rf,rd->fd/dot_general | solution.py:156
  490.5 6.6 reduce-scatter.15.cloned.1.call-done
  497.1 4.4 fusion.59
  501.5 68.7 %reduce-scatter.13.cloned.1.call-done = bf16[384,2048]{1,0:T(8,128)(2,1)} async-done(((bf16[1536,2048]{1,0:T(8,128)(2,1)}), bf16[384,2048]{1,0:T(8,128)(2,1)}) %reduce-scatter.13.cloned.1.call-update) | async-done | bytes 1572880 | tf_op jit(solution)/shard_map/reduce_scatter | solution.py:151
  570.2 5.5 fusion.90
  579.2 2.8 fusion.120
  582.0 32.3 %collective-permute-done = bf16[1,384,2048]{2,1,0:T(8,128)(2,1)} collective-permute-done((bf16[1,384,2048]{2,1,0:T(8,128)(2,1)}, bf16[1,384,2048]{2,1,0:T(8,128)(2,1)}, u32[]{:S(2)}, u32[]{:S(2)}) %collective-permute-start) | collective-permute-done | bytes 1572896 | tf_op jit(solution)/shard_map/ppermute | solution.py:23
  616.0 3.8 fusion.67
  621.2 68.0 %collective-permute-done.1 = bf16[2,384,2048]{2,1,0:T(8,128)(2,1)} collective-permute-done((bf16[2,384,2048]{2,1,0:T(8,128)(2,1)}, bf16[2,384,2048]{2,1,0:T(8,128)(2,1)}, u32[]{:S(2)}, u32[]{:S(2)}) %collective-permute-start.1) | collective-permute-done | bytes 3145760 | tf_op jit(solution)/shard_map/ppermute | solution.py:23
  689.1 3.5 pad_maximum_fusion
  694.9 2.7 copy-done.14
  697.6 5.3 convolution_convert_fusion.10
  702.8 3.5 reshape.222
  706.4 8.2 convolution_convert_fusion.7
  719.3 98.4 %while.27 = (s32[]{:T(128)}, bf16[2,768,4,128]{3,2,1,0:T(4,128)(2,1)}, bf16[2,768,4,128]{3,2,1,0:T(4,128)(2,1)}, bf16[2,768,4,128]{3,2,1,0:T(4,128)(2,1)}, bf16[...) while((s32[]{:T(128)}, ...), condition=%wide.region_15.16_spmd, body=%wide.region_13.15_spmd.sunk | while | flops 3051156480 | bytes 169179440 | solution.py:182
  725.2 3.6 copy-done.1
  728.9 3.5 fusion.152
  734.6 8.1 multiply_reduce_fusion.3
  742.7 10.9 %multiply_convert_fusion.7 = bf16[4,768,768]{1,2,0:T(8,128)(2,1)} fusion(f32[4,768,768]{1,2,0:T(8,128)} %get-tuple-element.306, f32[4,768,768]{1,2,0:T(8,128)} %copy-done.1, f32[4,768]{1,0:T(4,128)S(1)} %get-tuple-element.307, f32[4,768]{1,0:T(4,128)S(1)} %dynamic-slice_bitcast_fusion.2, pred[768,768]{0,1:T(8,128)(4,1)S(1)} %fusion.150), kind=kLoop, calls=%fused_computation.21.clone.1 | loop fusion | flops 11796480 | bytes 24207360 | tf_op jit(solution)/shard_map/while/body/eval_jaxpr/convert_element_type | solution.py:91
  753.5 4.4 fusion.153
  765.5 3.1 constant_dynamic-update-slice_fusion.9
  774.4 3.6 copy-done.1
  778.1 3.5 fusion.152
  783.8 8.0 multiply_reduce_fusion.3
  791.8 10.7 %multiply_convert_fusion.7 = bf16[4,768,768]{1,2,0:T(8,128)(2,1)} fusion(f32[4,768,768]{1,2,0:T(8,128)} %get-tuple-element.306, f32[4,768,768]{1,2,0:T(8,128)} %copy-done.1, f32[4,768]{1,0:T(4,128)S(1)} %get-tuple-element.307, f32[4,768]{1,0:T(4,128)S(1)} %dynamic-slice_bitcast_fusion.2, pred[768,768]{0,1:T(8,128)(4,1)S(1)} %fusion.150), kind=kLoop, calls=%fused_computation.21.clone.1 | loop fusion | flops 11796480 | bytes 24207360 | tf_op jit(solution)/shard_map/while/body/eval_jaxpr/convert_element_type | solution.py:91
  802.5 4.4 fusion.153
  814.5 3.1 constant_dynamic-update-slice_fusion.9
  817.7 8.0 multiply_convert_fusion.2
  825.8 8.0 convolution_convert_fusion.8
  833.9 8.1 convolution_convert_fusion.9
  842.3 10.2 fusion.74
  852.5 6.4 fusion.71
  859.0 15.7 %add_convert_fusion = bf16[1536,2048]{1,0:T(8,128)(2,1)} fusion(f32[1536,2048]{1,0:T(8,128)} %fusion.71, f32[1536,2048]{1,0:T(8,128)} %fusion.74, bf16[2048,512]{1,0:T(8,128)(2,1)} %param.17, bf16[192,8,4,128]{3,2,1,0:T(4,128)(2,1)} %bitcast.158), kind=kOutput, calls=%fused_computation.69 | convolution fusion | flops 3233808384 | bytes 35127296 | tf_op jit(solution)/shard_map/dot_general | solution.py:51
  874.7 2.8 convert_element_type.158
  877.5 2.7 convert_element_type.160
  883.9 14.8 %reduce-scatter.23.cloned.1.call-done = bf16[256,512]{1,0:T(8,128)(2,1)} async-done(((bf16[2048,512]{1,0:T(8,128)(2,1)}), bf16[256,512]{1,0:T(8,128)(2,1)}) %reduce-scatter.23.cloned.1.call-update) | async-done | bytes 262160 | tf_op jit(solution)/shard_map/reduce_scatter | solution.py:230
  900.5 34.9 %reduce-scatter.21.cloned.1.call-done = bf16[256,512]{1,0:T(8,128)(2,1)} async-done(((bf16[2048,512]{1,0:T(8,128)(2,1)}), bf16[256,512]{1,0:T(8,128)(2,1)}) %reduce-scatter.21.cloned.1.call-update) | async-done | bytes 262160 | tf_op jit(solution)/shard_map/reduce_scatter | solution.py:227
  937.2 70.0 %reduce-scatter.17.cloned.1.call-done = bf16[384,2048]{1,0:T(8,128)(2,1)} async-done(((bf16[1536,2048]{1,0:T(8,128)(2,1)}), bf16[384,2048]{1,0:T(8,128)(2,1)}) %reduce-scatter.17.cloned.1.call-update) | async-done | bytes 1572880 | tf_op jit(solution)/shard_map/reduce_scatter | solution.py:199
  1007.1 2.8 fusion.62
  1011.6 39.5 %all-reduce = (f32[2048]{0:T(1024)}, f32[2048]{0:T(1024)}) all-reduce(f32[2048]{0:T(1024)S(1)} %get-tuple-element.143, f32[2048]{0:T(1024)S(1)} %copy-done.33), channel_id=1, replica_groups=mesh['dp'=8,'mp'=4] {'dp','mp'}, use_global_device_ids=true, to_apply=%region_26.27 | all-reduce | flops 4096 | bytes 32768 | tf_op jit(solution)/shard_map/psum | solution.py:215
  1051.1 5.1 add_add_fusion.2
  (190 shorter events, 85.1 us)
Async XLA Ops:
  7.2 148.7 %copy-start = (bf16[512,2048]{1,0:T(8,128)(2,1)S(1)}, bf16[512,2048]{1,0:T(8,128)(2,1)}, u32[]{:S(2)}) copy-start(bf16[512,2048]{1,0:T(8,128)(2,1)} %param.20) | copy-start | bytes 6291460
  7.2 5.1 copy-start.21
  7.2 79.8 %all-gather.4.cloned.1.call-start = ((), (), s32[]{:S(2)}) async-start(), calls=%async_computation.10 | async-start | bytes 7864320 | tf_op jit(solution)/shard_map/all_gather | solution.py:124
  7.2 5.0 copy-start.3
  9.1 2.6 copy-start.23
  11.1 0.6 copy-start.36
  11.7 0.6 copy-start.29
  14.0 219.4 %reduce-scatter.11.cloned.1.call-start = ((), (), s32[]{:S(2)}) async-start(), calls=%async_computation.11 | async-start | bytes 7864320 | tf_op jit(solution)/shard_map/reduce_scatter | solution.py:139
  98.7 2.9 copy-start.15
  112.4 2.9 copy-start.40
  122.6 5.1 copy-start.19
  133.7 1.8 copy-start.12
  147.7 1.8 copy-start.12
  155.8 7.2 copy-start.17
  163.0 142.4 %all-gather.8.cloned.1.call-start = ((), (), s32[]{:S(2)}) async-start(), calls=%async_computation.14 | async-start | bytes 7864320 | tf_op jit(solution)/shard_map/all_gather | solution.py:155
  163.1 75.0 %copy-start.25 = (f32[2048]{0:T(1024)S(1)}, f32[2048]{0:T(1024)}, u32[]{:S(2)}) copy-start(f32[2048]{0:T(1024)} %param.24) | copy-start | bytes 24580
  163.8 214.1 %all-gather.6.cloned.1.call-start = ((), (), s32[]{:S(2)}) async-start(), calls=%async_computation.12 | async-start | bytes 7864320 | tf_op jit(solution)/shard_map/all_gather | solution.py:147
  233.4 2.5 copy-start.4
  233.4 2.8 copy-start.10
  236.2 1.3 copy-start.27
  236.9 0.6 copy-start.38
  237.5 0.6 copy-start.34
  240.0 257.1 %reduce-scatter.15.cloned.1.call-start = ((), (), s32[]{:S(2)}) async-start(), calls=%async_computation.15 | async-start | bytes 7864320 | tf_op jit(solution)/shard_map/reduce_scatter | solution.py:166
  426.7 143.5 %reduce-scatter.13.cloned.1.call-start = ((), (), s32[]{:S(2)}) async-start(), calls=%async_computation.13 | async-start | bytes 7864320 | tf_op jit(solution)/shard_map/reduce_scatter | solution.py:151
  447.3 427.4 %reduce-scatter.27.cloned.1.call-start = ((), (), s32[]{:S(2)}) async-start(), calls=%async_computation.21 | async-start | bytes 9437184 | tf_op jit(solution)/shard_map/reduce_scatter | solution.py:236
  467.4 410.2 %reduce-scatter.29.cloned.1.call-start = ((), (), s32[]{:S(2)}) async-start(), calls=%async_computation.22 | async-start | bytes 9437184 | tf_op jit(solution)/shard_map/reduce_scatter | solution.py:239
  490.1 7.0 copy-start.26
  490.1 7.0 copy-start.28
  490.1 7.0 copy-start.35
  490.1 11.4 %copy-start.39 = (f32[384]{0:T(512)S(1)}, f32[384]{0:T(512)}, u32[]{:S(2)}) copy-start(f32[384]{0:T(512)} %copy-done.38) | copy-start | bytes 4612
  490.1 390.2 %reduce-scatter.25.cloned.1.call-start = ((), (), s32[]{:S(2)}) async-start(), calls=%async_computation.20 | async-start | bytes 2359296 | tf_op jit(solution)/shard_map/reduce_scatter | solution.py:233
  570.2 5.5 copy-start.11
  575.7 2.2 copy-start.9
  575.7 3.5 copy-start.31
  577.9 36.5 %collective-permute-start = (bf16[1,384,2048]{2,1,0:T(8,128)(2,1)}, bf16[1,384,2048]{2,1,0:T(8,128)(2,1)}, u32[]{:S(2)}, u32[]{:S(2)}) collective-permute-start(bf16[1,384,2048]{2,1,0:T(8,128)(2,1)} %fusion.121), channel_id=1, source_target_pairs={{0,1},{1,0},{2,3},{3,2},{4,5},{5,4},{6,7},{7,6},{8,9},{9,8},{10,11... | collective-permute-start | bytes 4718600 | tf_op jit(solution)/shard_map/ppermute | solution.py:23
  619.8 69.3 %collective-permute-start.1 = (bf16[2,384,2048]{2,1,0:T(8,128)(2,1)}, bf16[2,384,2048]{2,1,0:T(8,128)(2,1)}, u32[]{:S(2)}, u32[]{:S(2)}) collective-permute-start(bf16[2,384,2048]{2,1,0:T(8,128)(2,1)} %get-tuple-element.190), channel_id=1, source_target_pairs={{0,2},{1,3},{2,0},{3,1},{4,6},{5,7},{6,4},{7,5},{8,10},{9,11},{10,... | collective-permute-start | bytes 9437192 | tf_op jit(solution)/shard_map/ppermute | solution.py:23
  694.9 2.7 copy-start.14
  714.5 4.7 copy-start.18
  714.5 4.7 copy-start.20
  714.6 167.5 %reduce-scatter.19.cloned.1.call-start = ((), (), s32[]{:S(2)}) async-start(), calls=%async_computation.17 | async-start | bytes 2359296 | tf_op jit(solution)/shard_map/reduce_scatter | solution.py:224
  719.4 4.4 copy-start.6
  719.4 4.4 copy-start.8
  725.2 3.7 copy-start.1
  753.5 4.4 copy-start.2
  753.5 4.5 copy-start.7
  768.7 4.4 copy-start.6
  768.7 4.4 copy-start.8
  774.4 3.7 copy-start.1
  802.5 4.4 copy-start.2
  802.5 4.5 copy-start.7
  825.8 72.9 %reduce-scatter.23.cloned.1.call-start = ((), (), s32[]{:S(2)}) async-start(), calls=%async_computation.19 | async-start | bytes 2359296 | tf_op jit(solution)/shard_map/reduce_scatter | solution.py:230
  833.8 101.5 %reduce-scatter.21.cloned.1.call-start = ((), (), s32[]{:S(2)}) async-start(), calls=%async_computation.18 | async-start | bytes 2359296 | tf_op jit(solution)/shard_map/reduce_scatter | solution.py:227
  842.0 165.1 %reduce-scatter.17.cloned.1.call-start = ((), (), s32[]{:S(2)}) async-start(), calls=%async_computation.16 | async-start | bytes 7864320 | tf_op jit(solution)/shard_map/reduce_scatter | solution.py:199
  842.3 10.2 copy-start.16
  842.3 10.2 copy-start.41
  877.5 129.6 %copy-start.22 = (f32[2048]{0:T(1024)S(1)}, f32[2048]{0:T(1024)}, u32[]{:S(2)}) copy-start(f32[2048]{0:T(1024)} %param.23) | copy-start | bytes 24580
  877.5 129.6 %copy-start.24 = (f32[384]{0:T(512)S(1)}, f32[384]{0:T(512)}, u32[]{:S(2)}) copy-start(f32[384]{0:T(512)} %copy-done.23) | copy-start | bytes 4612
  880.3 129.7 %copy-start.37 = (f32[384]{0:T(512)S(1)}, f32[384]{0:T(512)}, u32[]{:S(2)}) copy-start(f32[384]{0:T(512)} %copy-done.36) | copy-start | bytes 4612
  880.3 129.7 %copy-start.30 = (f32[384]{0:T(512)S(1)}, f32[384]{0:T(512)}, u32[]{:S(2)}) copy-start(f32[384]{0:T(512)} %copy-done.29) | copy-start | bytes 4612
  937.2 74.4 %copy-start.33 = (f32[2048]{0:T(1024)S(1)}, f32[2048]{0:T(1024)}, u32[]{:S(2)}) copy-start(f32[2048]{0:T(1024)} %get-tuple-element.141) | copy-start | bytes 24580
  937.2 113.9 %copy-start.32 = (f32[384]{0:T(512)S(1)}, f32[384]{0:T(512)}, u32[]{:S(2)}) copy-start(f32[384]{0:T(512)} %copy-done.31) | copy-start | bytes 4612
  1007.1 2.8 copy-start.5
  1007.1 2.8 copy-start.13
Sparse Core Ops, SparseCore 0:
  14.1 72.8 all-gather.3
  163.2 70.2 reduce-scatter.10
  235.3 70.1 all-gather.7
  307.7 70.1 all-gather.5
  426.9 70.2 reduce-scatter.14
  499.9 70.2 reduce-scatter.12
  572.5 89.5 reduce-scatter.26
  664.4 87.9 reduce-scatter.28
  754.7 34.1 reduce-scatter.24
  825.9 35.9 reduce-scatter.18
  864.1 34.4 reduce-scatter.22
  900.8 34.5 reduce-scatter.20
  938.3 68.7 reduce-scatter.16
